TPU v7x, 32 devices: a whole 2x2x4 slice. The times are simulated.
32 devices in a mesh: dp: 8 (over z, core), expert: 4 (over y, x).
Axes of the slice: x: 2, y: 2, z: 4, core: 2. Of those that a mesh axis runs over, the one named last changes fastest.
Arguments:
- tokens: bfloat16 [4096, 2048], P(('dp', 'expert')), may hold values from -6 to 6
- expert_ids: int32 [4096, 8], P(('dp', 'expert')), may hold values from 0 to 127, as said below
- gate_probs: float32 [4096, 8], P(('dp', 'expert')), may hold values from 0.1 to 1
- cotangent: bfloat16 [4096, 2048], P(('dp', 'expert')), may hold values from -1.5 to 1.5
- expert_weights: bfloat16 [2048, 4, 3, 768], P(None, 'expert'), may hold values from -0.21875 to 0.21875
Outputs:
- mixed: bfloat16 [4096, 2048], P(('dp', 'expert'))
- grad_tokens: bfloat16 [4096, 2048], P(('dp', 'expert'))
- grad_gates: float32 [4096, 8], P(('dp', 'expert'))
- grad_weights: bfloat16 [2048, 4, 3, 768], P('dp', 'expert')
Inputs may be any that keep to these rules, and one draw needn't show every extreme that they name: `expert_ids`: each row names 8 different experts. In the rows of one device every expert below 4 is named by 1 to 24 rows, and for every index of dp some such expert is named by exactly 24 rows of each device of that index.
All inputs are finite; a program needn't handle non-finite values.
Results may differ from a plain program's by a relative error of at most 0.0058.
Values may be sent and summed in bfloat16 or wider, within the bound.
No kernel may reach another device: no remote copies, remote signals or barrier semaphores. Data moves between devices by JAX's collectives and lax.ppermute only.
A program may use at most 128 MiB of HBM per device.

v0:
```python
import jax
import jax.numpy as jnp
from jax import lax
from jax.sharding import PartitionSpec as P

BLOCK = 128
CAP = 24


def expert_rows(x_rows, dy_rows, weights):
    w_gate = weights[:, 0, :]
    w_up = weights[:, 1, :]
    w_down = weights[:, 2, :]
    contract_last = (((1,), (1,)), ((), ()))
    gate_proj = jnp.dot(x_rows, w_gate, preferred_element_type=jnp.float32)
    up_proj = jnp.dot(x_rows, w_up, preferred_element_type=jnp.float32)
    sigmoid_gate = jax.nn.sigmoid(gate_proj)
    silu_gate = gate_proj * sigmoid_gate
    hidden = (silu_gate * up_proj).astype(jnp.bfloat16)
    expert_out = lax.dot_general(
        hidden, w_down, contract_last, preferred_element_type=jnp.float32
    ).astype(jnp.bfloat16)
    hidden_grad = jnp.dot(dy_rows, w_down, preferred_element_type=jnp.float32)
    gate_grad = (
        hidden_grad * up_proj * sigmoid_gate * (1.0 + gate_proj * (1.0 - sigmoid_gate))
    ).astype(jnp.bfloat16)
    up_grad = (hidden_grad * silu_gate).astype(jnp.bfloat16)
    token_part = (
        lax.dot_general(gate_grad, w_gate, contract_last, preferred_element_type=jnp.float32)
        + lax.dot_general(up_grad, w_up, contract_last, preferred_element_type=jnp.float32)
    ).astype(jnp.bfloat16)
    return (expert_out, token_part, hidden, gate_grad, up_grad)


def squeeze_live(rows_x, rows_dy):
    total_rows = rows_x.shape[0]
    padded_rows = -(-total_rows // BLOCK) * BLOCK
    is_live = jnp.any(rows_x != 0, axis=1)
    live_count = is_live.astype(jnp.int32)
    live_total = jnp.sum(live_count)
    placement = jnp.where(
        is_live, jnp.cumsum(live_count) - 1, live_total + jnp.cumsum(1 - live_count) - 1
    )
    source_row = (
        jnp.zeros((padded_rows,), jnp.int32)
        .at[placement]
        .set(jnp.arange(total_rows, dtype=jnp.int32))
    )
    keep_row = (jnp.arange(padded_rows) < live_total)[:, None]
    packed_x = jnp.where(keep_row, rows_x[source_row], jnp.zeros((), rows_x.dtype))
    packed_dy = jnp.where(keep_row, rows_dy[source_row], jnp.zeros((), rows_dy.dtype))
    return (packed_x, packed_dy, placement, live_total)


def run_expert(rows_x, rows_dy, weights):
    packed_x, packed_dy, placement, live_total = squeeze_live(rows_x, rows_dy)
    padded_rows, model_width = packed_x.shape
    hidden_units = weights.shape[2]
    block_total = (live_total + BLOCK - 1) // BLOCK

    def block_step(block_index, state_in):
        row_start = block_index * BLOCK
        x_block = lax.dynamic_slice_in_dim(packed_x, row_start, BLOCK, 0)
        dy_block = lax.dynamic_slice_in_dim(packed_dy, row_start, BLOCK, 0)
        results = expert_rows(x_block, dy_block, weights)
        return tuple(
            (
                lax.dynamic_update_slice_in_dim(full_array, block_part, row_start, 0)
                for full_array, block_part in zip(state_in, results)
            )
        )

    initial = (
        jnp.zeros((padded_rows, model_width), jnp.bfloat16),
        jnp.zeros((padded_rows, model_width), jnp.bfloat16),
        jnp.zeros((padded_rows, hidden_units), jnp.bfloat16),
        jnp.zeros((padded_rows, hidden_units), jnp.bfloat16),
        jnp.zeros((padded_rows, hidden_units), jnp.bfloat16),
    )
    out_all, part_all, hidden_all, gate_all, up_all = lax.fori_loop(
        0, block_total, block_step, initial
    )
    contract_first = (((0,), (0,)), ((), ()))
    groups = lax.axis_size("dp")
    width_part = model_width // groups
    split_x = packed_x.reshape(padded_rows, groups, width_part)
    split_dy = packed_dy.reshape(padded_rows, groups, width_part)
    recv_x, recv_dy = (
        lax.all_to_all(split_x, "dp", split_axis=1, concat_axis=0, tiled=True),
        lax.all_to_all(split_dy, "dp", split_axis=1, concat_axis=0, tiled=True),
    )
    recv_x = recv_x.reshape(groups * padded_rows, width_part)
    recv_dy = recv_dy.reshape(groups * padded_rows, width_part)
    gate_piece = lax.all_gather(gate_all, "dp", axis=0, tiled=True)
    up_piece = lax.all_gather(up_all, "dp", axis=0, tiled=True)
    hidden_piece = lax.all_gather(hidden_all, "dp", axis=0, tiled=True)
    gate_term = lax.dot_general(
        recv_x, gate_piece, contract_first, preferred_element_type=jnp.float32
    )
    up_term = lax.dot_general(recv_x, up_piece, contract_first, preferred_element_type=jnp.float32)
    down_term = lax.dot_general(
        recv_dy, hidden_piece, contract_first, preferred_element_type=jnp.float32
    )
    folded = jnp.stack([gate_term, up_term, down_term], axis=1)
    summed = folded[:, None, :, :]
    return (out_all[placement], part_all[placement], summed)


def per_device(tokens, expert_ids, gate_probs, cotangent, expert_weights):
    tok_rows, model_width = tokens.shape
    top_count = expert_ids.shape[1]
    held_count = lax.axis_size("expert")
    slot_total = held_count * CAP
    flat_ids = expert_ids.reshape(-1)
    is_held = flat_ids < held_count
    onehot = (flat_ids[:, None] == jnp.arange(held_count, dtype=jnp.int32)[None, :]).astype(
        jnp.int32
    )
    position = jnp.sum(jnp.cumsum(onehot, axis=0) * onehot, axis=1) - 1
    destination = jnp.where(is_held, flat_ids * CAP + position, slot_total)
    source_token = jnp.arange(tok_rows * top_count, dtype=jnp.int32) // top_count
    slot_token = jnp.zeros((slot_total,), jnp.int32).at[destination].set(source_token, mode="drop")
    slot_prob = (
        jnp.zeros((slot_total,), jnp.float32)
        .at[destination]
        .set(gate_probs.reshape(-1), mode="drop")
    )
    slot_live = jnp.zeros((slot_total,), jnp.bool_).at[destination].set(True, mode="drop")
    send_x = jnp.where(slot_live[:, None], tokens[slot_token], jnp.zeros((), jnp.bfloat16))
    send_dy = (slot_prob[:, None] * cotangent[slot_token].astype(jnp.float32)).astype(jnp.bfloat16)
    recv_x, recv_dy = (
        lax.all_to_all(
            send_x.reshape(held_count, CAP, model_width),
            "expert",
            split_axis=0,
            concat_axis=0,
            tiled=True,
        ),
        lax.all_to_all(
            send_dy.reshape(held_count, CAP, model_width),
            "expert",
            split_axis=0,
            concat_axis=0,
            tiled=True,
        ),
    )
    rows_x = recv_x.reshape(slot_total, model_width)
    rows_dy = recv_dy.reshape(slot_total, model_width)
    weights = expert_weights[:, 0]
    out_rows, part_rows, summed = run_expert(rows_x, rows_dy, weights)
    back_out, back_part = (
        lax.all_to_all(
            out_rows.reshape(held_count, CAP, model_width),
            "expert",
            split_axis=0,
            concat_axis=0,
            tiled=True,
        ),
        lax.all_to_all(
            part_rows.reshape(held_count, CAP, model_width),
            "expert",
            split_axis=0,
            concat_axis=0,
            tiled=True,
        ),
    )
    safe_slot = jnp.where(is_held, destination, 0)
    took_out = jnp.where(
        is_held[:, None],
        back_out.reshape(slot_total, model_width)[safe_slot].astype(jnp.float32),
        jnp.zeros((), jnp.float32),
    ).reshape(tok_rows, top_count, model_width)
    took_part = jnp.where(
        is_held[:, None],
        back_part.reshape(slot_total, model_width)[safe_slot].astype(jnp.float32),
        jnp.zeros((), jnp.float32),
    ).reshape(tok_rows, top_count, model_width)
    mixed_out = jnp.sum(gate_probs[:, :, None] * took_out, axis=1).astype(jnp.bfloat16)
    grad_gates = jnp.sum(took_out * cotangent.astype(jnp.float32)[:, None, :], axis=2)
    grad_tokens = jnp.sum(took_part, axis=1).astype(jnp.bfloat16)
    return (mixed_out, grad_tokens, grad_gates, summed.astype(jnp.bfloat16))


def solution(mesh):
    in_specs = (
        P(("dp", "expert"), None),
        P(("dp", "expert"), None),
        P(("dp", "expert"), None),
        P(("dp", "expert"), None),
        P(None, "expert", None, None),
    )
    out_specs = (
        P(("dp", "expert"), None),
        P(("dp", "expert"), None),
        P(("dp", "expert"), None),
        P("dp", "expert", None, None),
    )
    return jax.shard_map(
        per_device, mesh=mesh, in_specs=in_specs, out_specs=out_specs, check_vma=False
    )
```

profile of v0, /device:TPU:0, one launch (start us, length us, event | category | flops | bytes accessed | tf_op | source)
XLA Modules:
  0.0 165.4 jit_solution(4226696876934039421)
XLA Ops:
  12.3 4.3 %scatter_custom_fusion.1 = s32[96]{0:T(128)S(1)} fusion(s32[1024]{0:T(1024)S(1)} %bitcast.105, s32[1024]{0:T(1024)S(1)} %add_select_fusion, s32[]{:T(128)} %copy.53), kind=kCustom, calls=%fused_computation.100 | custom fusion | bytes 388 | tf_op jit(solution)/shard_map/scatter | solution.py:122
  16.7 4.3 %scatter_custom_fusion = pred[96]{0:T(512)(128)(4,1)S(1)} fusion(s32[1024]{0:T(1024)S(1)} %bitcast.106, pred[1024]{0:T(1024)(128)(4,1)S(1)} %broadcast.259, pred[]{:T(512)} %constant.84.clone.1), kind=kCustom, calls=%fused_computation.92 | custom fusion | bytes 97 | tf_op jit(solution)/shard_map/scatter | solution.py:128
  22.8 5.2 %all-to-all-start = ((bf16[4,24,2048]{2,1,0:T(8,128)(2,1)}), bf16[4,24,2048]{2,1,0:T(8,128)(2,1)S(1)}, u32[]{:S(2)}, u32[]{:S(2)}) async-start(bf16[4,24,2048]{2,1,0:T(8,128)(2,1)} %broadcast_select_fusion.1), calls=%async_computation | async-start | bytes 786432 | tf_op jit(solution)/shard_map/all_to_all | solution.py:132
  29.1 4.3 %scatter_custom_fusion.3 = f32[96]{0:T(128)S(1)} fusion(s32[1024]{0:T(1024)S(1)} %bitcast.107, f32[1024]{0:T(1024)S(1)} %reshape.410, f32[]{:T(128)} %constant.94.clone.1), kind=kCustom, calls=%fused_computation.95 | custom fusion | bytes 388 | tf_op jit(solution)/shard_map/scatter | solution.py:126
  34.6 3.9 %all-to-all-start.1 = ((bf16[4,24,2048]{2,1,0:T(8,128)(2,1)}), bf16[4,24,2048]{2,1,0:T(8,128)(2,1)S(1)}, u32[]{:S(2)}, u32[]{:S(2)}) async-start(bf16[4,24,2048]{2,1,0:T(8,128)(2,1)} %fusion.18), calls=%async_computation.1 | async-start | bytes 786432 | tf_op jit(solution)/shard_map/all_to_all | solution.py:139
  44.2 2.7 %negate_exponential_fusion = (f32[128,768]{1,0:T(8,128)S(1)}, f32[128,768]{1,0:T(8,128)S(1)}) fusion(bf16[2048,3,768]{2,0,1:T(8,128)(2,1)} %bitcast.108, bf16[128,2048]{1,0:T(8,128)(2,1)S(1)} %gather_fusion.1, pred[128]{0:T(512)(128)(4,1)S(1)} %iota_compare_fusion.2), kind=kOutput, calls=%fused_computation.56 | convolution fusion | flops 403013632 | bytes 4456576 | tf_op jit(solution)/shard_map/while/body/dot_general | solution.py:15
  50.4 3.5 %fusion.46 = (f32[128,768]{1,0:T(8,128)S(1)}, f32[128,768]{1,0:T(8,128)}) fusion(f32[128,768]{1,0:T(8,128)S(1)} %fusion.9, bf16[2048,3,768]{2,0,1:T(8,128)(2,1)} %bitcast.110, bf16[128,2048]{1,0:T(8,128)(2,1)S(1)} %gather_fusion.3, pred[128]{0:T(512)(128)(4,1)S(1)} %iota_compare_fusion.2), kind=kOutput, calls=%fused_computation.108 | convolution fusion | flops 403013632 | bytes 4849792 | tf_op jit(solution)/shard_map/while/body/dot_general | solution.py:23
  53.9 3.2 %fusion.14 = bf16[128,2048]{1,0:T(8,128)(2,1)S(1)} fusion(bf16[2048,3,768]{2,0,1:T(8,128)(2,1)} %bitcast.111, f32[128,768]{1,0:T(8,128)S(1)} %fusion.9, f32[128,768]{1,0:T(8,128)S(1)} %get-tuple-element.446), kind=kOutput, calls=%fused_computation.36 | convolution fusion | flops 403505152 | bytes 4456448 | tf_op jit(solution)/shard_map/while/body/dot_general | solution.py:20
  57.1 4.0 %fusion.6 = f32[128,2048]{1,0:T(8,128)} fusion(bf16[2048,3,768]{2,0,1:T(8,128)(2,1)} %bitcast.112, f32[128,768]{1,0:T(8,128)S(1)} %get-tuple-element.446, f32[128,768]{1,0:T(8,128)S(1)} %get-tuple-element.448), kind=kOutput, calls=%fused_computation.28 | convolution fusion | flops 403537920 | bytes 4980736 | tf_op jit(solution)/shard_map/while/body/dot_general | solution.py:29
  61.1 3.4 %fusion.13 = bf16[128,2048]{1,0:T(8,128)(2,1)S(1)} fusion(f32[128,2048]{1,0:T(8,128)} %fusion.6, bf16[2048,3,768]{2,0,1:T(8,128)(2,1)} %bitcast.113, f32[128,768]{1,0:T(8,128)} %get-tuple-element.449, f32[128,768]{1,0:T(8,128)S(1)} %get-tuple-element.446), kind=kOutput, calls=%fused_computation.35 | convolution fusion | flops 403767296 | bytes 5505024 | tf_op jit(solution)/shard_map/while/body/dot_general | solution.py:30
  68.3 3.7 %while.24 = (s32[]{:T(128)}, bf16[128,2048]{1,0:T(8,128)(2,1)}, bf16[128,2048]{1,0:T(8,128)(2,1)}, bf16[128,768]{1,0:T(8,128)(2,1)}, bf16[128,768]{1,0:T(8,128)(...) while((s32[]{:T(128)}, bf16[128,2048]{1,0:T(8,128)(2,1)}, ...), condition=%wide.region_12.13_spmd, body=%wide.region_11.12_spmd.sunk | while | flops 1277954 | bytes 4653197 | solution.py:80
  72.8 3.2 %gather_fusion.4 = bf16[96,2048]{1,0:T(8,128)(2,1)} fusion(bf16[128,2048]{1,0:T(8,128)(2,1)} %get-tuple-element.306, s32[1024]{0:T(1024)S(1)} %pad_clamp_fusion), kind=kCustom, calls=%fused_computation.4 | custom fusion | bytes 786816 | tf_op jit(solution)/shard_map/gather | solution.py:106
  76.0 4.2 %all-to-all-start.2 = ((bf16[4,24,2048]{2,1,0:T(8,128)(2,1)}), bf16[4,24,2048]{2,1,0:T(8,128)(2,1)S(1)}, u32[]{:S(2)}, u32[]{:S(2)}) async-start(bf16[4,24,2048]{2,1,0:T(8,128)(2,1)} %bitcast.11), calls=%async_computation.2 | async-start | bytes 786432 | tf_op jit(solution)/shard_map/all_to_all | solution.py:152
  82.5 3.6 %all-to-all-done.2 = bf16[4,24,2048]{2,1,0:T(8,128)(2,1)S(1)} async-done(((bf16[4,24,2048]{2,1,0:T(8,128)(2,1)}), bf16[4,24,2048]{2,1,0:T(8,128)(2,1)S(1)}, u32[]{:S(2)}, u32[]{:S(2)}) %all-to-all-start.2) | async-done | bytes 393248 | tf_op jit(solution)/shard_map/all_to_all | solution.py:152
  86.0 3.5 %all-to-all-start.3 = ((bf16[4,24,2048]{2,1,0:T(8,128)(2,1)}), bf16[4,24,2048]{2,1,0:T(8,128)(2,1)S(1)}, u32[]{:S(2)}, u32[]{:S(2)}) async-start(bf16[4,24,2048]{2,1,0:T(8,128)(2,1)} %bitcast.15), calls=%async_computation.3 | async-start | bytes 786432 | tf_op jit(solution)/shard_map/all_to_all | solution.py:159
  90.7 4.7 %all-to-all-done.3 = bf16[4,24,2048]{2,1,0:T(8,128)(2,1)S(1)} async-done(((bf16[4,24,2048]{2,1,0:T(8,128)(2,1)}), bf16[4,24,2048]{2,1,0:T(8,128)(2,1)S(1)}, u32[]{:S(2)}, u32[]{:S(2)}) %all-to-all-start.3) | async-done | bytes 393248 | tf_op jit(solution)/shard_map/all_to_all | solution.py:159
  95.3 4.9 %all-to-all-start.4 = ((bf16[128,8,256]{2,0,1:T(8,128)(2,1)}), bf16[128,8,256]{2,0,1:T(8,128)(2,1)S(1)}, u32[]{:S(2)}, u32[]{:S(2)}) async-start(bf16[128,8,256]{2,0,1:T(8,128)(2,1)} %get-tuple-element.350), calls=%async_computation.4 | async-start | bytes 1048576 | tf_op jit(solution)/shard_map/all_to_all | solution.py:89
  100.5 6.0 %gather_fusion.5 = bf16[1024,2048]{1,0:T(8,128)(2,1)} fusion(bf16[96,2048]{1,0:T(8,128)(2,1)S(1)} %bitcast.91, s32[1024]{0:T(1024)S(1)} %broadcast_clamp_fusion), kind=kCustom, calls=%fused_computation.5 | custom fusion | bytes 8392704 | tf_op jit(solution)/shard_map/gather | solution.py:170
  106.5 6.0 %gather_fusion.7 = bf16[1024,2048]{1,0:T(8,128)(2,1)} fusion(bf16[96,2048]{1,0:T(8,128)(2,1)S(1)} %bitcast.92, s32[1024]{0:T(1024)S(1)} %broadcast_clamp_fusion), kind=kCustom, calls=%fused_computation.7 | custom fusion | bytes 8392704 | tf_op jit(solution)/shard_map/gather | solution.py:175
  112.5 3.3 %fusion.4 = f32[1024]{0:T(1024)S(1)} fusion(bf16[1024,2048]{1,0:T(8,128)(2,1)} %gather_fusion.5, f32[128,2048]{1,0:T(8,128)S(1)} %convert_element_type.142, pred[1024]{0:T(1024)(128)(4,1)S(1)} %broadcast_in_dim.103), kind=kLoop, calls=%fused_computation.22 | loop fusion | flops 8387584 | bytes 5248000 | tf_op jit(solution)/shard_map/reduce_sum | solution.py:179
  116.5 5.3 %all-to-all-done.4 = bf16[128,8,256]{2,0,1:T(8,128)(2,1)S(1)} async-done(((bf16[128,8,256]{2,0,1:T(8,128)(2,1)}), bf16[128,8,256]{2,0,1:T(8,128)(2,1)S(1)}, u32[]{:S(2)}, u32[]{:S(2)}) %all-to-all-start.4) | async-done | bytes 524320 | tf_op jit(solution)/shard_map/all_to_all | solution.py:89
  121.8 3.7 %all-to-all-start.5 = ((bf16[128,8,256]{2,0,1:T(8,128)(2,1)}), bf16[128,8,256]{2,0,1:T(8,128)(2,1)S(1)}, u32[]{:S(2)}, u32[]{:S(2)}) async-start(bf16[128,8,256]{2,0,1:T(8,128)(2,1)} %get-tuple-element.351), calls=%async_computation.5 | async-start | bytes 1048576 | tf_op jit(solution)/shard_map/all_to_all | solution.py:90
  125.6 10.4 %fusion.5 = (bf16[128,2048]{1,0:T(8,128)(2,1)}, bf16[128,2048]{1,0:T(8,128)(2,1)}) fusion(bf16[1024,2048]{1,0:T(8,128)(2,1)} %gather_fusion.7, pred[128,8]{1,0:T(8,128)(4,1)S(1)} %copy.15, bf16[1024,2048]{1,0:T(8,128)(2,1)} %gather_fusion.5, f32[128,8]{1,0:T(8,128)S(1)} %copy-done.9), kind=kLoop, calls=%fused_computation.24 | loop fusion | flops 14155776 | bytes 9442304 | tf_op jit(solution)/shard_map/reduce_sum | solution.py:180
  140.6 15.1 %all-gather.8.cloned.1.call-done = bf16[1024,768]{1,0:T(8,128)(2,1)} async-done(((bf16[128,768]{1,0:T(8,128)(2,1)}), bf16[1024,768]{1,0:T(8,128)(2,1)}) %all-gather.8.cloned.1.call-update) | async-done | bytes 1572880 | tf_op jit(solution)/shard_map/all_gather | solution.py:96
  (103 shorter events, 38.0 us)
Async XLA Ops:
  7.2 14.0 %copy-start = (bf16[128,2048]{1,0:T(8,128)(2,1)S(1)}, bf16[128,2048]{1,0:T(8,128)(2,1)}, u32[]{:S(2)}) copy-start(bf16[128,2048]{1,0:T(8,128)(2,1)} %param.7) | copy-start | bytes 1572868
  7.2 20.8 %copy-start.1 = (bf16[128,2048]{1,0:T(8,128)(2,1)S(1)}, bf16[128,2048]{1,0:T(8,128)(2,1)}, u32[]{:S(2)}) copy-start(bf16[128,2048]{1,0:T(8,128)(2,1)} %param.10) | copy-start | bytes 1572868
  21.1 7.7 %copy-start.11 = (f32[128,8]{0,1:T(8,128)S(1)}, f32[128,8]{0,1:T(8,128)}, u32[]{:S(2)}) copy-start(f32[128,8]{0,1:T(8,128)} %param.9) | copy-start | bytes 12292
  22.8 11.8 %all-to-all-start = ((bf16[4,24,2048]{2,1,0:T(8,128)(2,1)}), bf16[4,24,2048]{2,1,0:T(8,128)(2,1)S(1)}, u32[]{:S(2)}, u32[]{:S(2)}) async-start(bf16[4,24,2048]{2,1,0:T(8,128)(2,1)} %broadcast_select_fusion.1), calls=%async_computation | async-start | bytes 786432 | tf_op jit(solution)/shard_map/all_to_all | solution.py:132
  29.0 15.2 %copy-start.8 = (f32[128,8]{1,0:T(8,128)}, f32[128,8]{1,0:T(8,128)S(1)}, u32[]{:S(2)}) copy-start(f32[128,8]{1,0:T(8,128)S(1)} %copy.14) | copy-start | bytes 12292
  34.6 14.8 %all-to-all-start.1 = ((bf16[4,24,2048]{2,1,0:T(8,128)(2,1)}), bf16[4,24,2048]{2,1,0:T(8,128)(2,1)S(1)}, u32[]{:S(2)}, u32[]{:S(2)}) async-start(bf16[4,24,2048]{2,1,0:T(8,128)(2,1)} %fusion.18), calls=%async_computation.1 | async-start | bytes 786432 | tf_op jit(solution)/shard_map/all_to_all | solution.py:139
  38.5 97.5 %all-gather.4.cloned.1.call-start = ((), (), s32[]{:S(2)}) async-start(), calls=%async_computation.6 | async-start | bytes 1769472 | tf_op jit(solution)/shard_map/all_gather | solution.py:94
  44.2 5.3 %copy-start.4 = (bf16[128,2048]{1,0:T(8,128)(2,1)}, bf16[128,2048]{1,0:T(8,128)(2,1)S(1)}, u32[]{:S(2)}) copy-start(bf16[128,2048]{1,0:T(8,128)(2,1)S(1)} %gather_fusion.1) | copy-start | bytes 1572868
  50.4 3.5 %copy-start.6 = (bf16[128,2048]{1,0:T(8,128)(2,1)}, bf16[128,2048]{1,0:T(8,128)(2,1)S(1)}, u32[]{:S(2)}) copy-start(bf16[128,2048]{1,0:T(8,128)(2,1)S(1)} %gather_fusion.3) | copy-start | bytes 1572868
  53.9 3.2 %copy-start.3 = (f32[128,768]{1,0:T(8,128)}, f32[128,768]{1,0:T(8,128)S(1)}, u32[]{:S(2)}) copy-start(f32[128,768]{1,0:T(8,128)S(1)} %get-tuple-element.448) | copy-start | bytes 1179652
  72.0 8.9 %copy-start.2 = (bf16[128,2048]{1,0:T(8,128)(2,1)S(1)}, bf16[128,2048]{1,0:T(8,128)(2,1)}, u32[]{:S(2)}) copy-start(bf16[128,2048]{1,0:T(8,128)(2,1)} %get-tuple-element.307) | copy-start | bytes 1572868
  72.0 66.1 %all-gather.6.cloned.1.call-start = ((), (), s32[]{:S(2)}) async-start(), calls=%async_computation.7 | async-start | bytes 1769472 | tf_op jit(solution)/shard_map/all_gather | solution.py:95
  72.8 16.7 %copy-start.5 = (bf16[128,2048]{1,0:T(8,128)(2,1)S(1)}, bf16[128,2048]{1,0:T(8,128)(2,1)}, u32[]{:S(2)}) copy-start(bf16[128,2048]{1,0:T(8,128)(2,1)} %copy-done.4) | copy-start | bytes 1572868
  72.8 16.7 %copy-start.7 = (bf16[128,2048]{1,0:T(8,128)(2,1)S(1)}, bf16[128,2048]{1,0:T(8,128)(2,1)}, u32[]{:S(2)}) copy-start(bf16[128,2048]{1,0:T(8,128)(2,1)} %copy-done.6) | copy-start | bytes 1572868
  76.0 10.1 %all-to-all-start.2 = ((bf16[4,24,2048]{2,1,0:T(8,128)(2,1)}), bf16[4,24,2048]{2,1,0:T(8,128)(2,1)S(1)}, u32[]{:S(2)}, u32[]{:S(2)}) async-start(bf16[4,24,2048]{2,1,0:T(8,128)(2,1)} %bitcast.11), calls=%async_computation.2 | async-start | bytes 786432 | tf_op jit(solution)/shard_map/all_to_all | solution.py:152
  80.2 75.5 %all-gather.8.cloned.1.call-start = ((), (), s32[]{:S(2)}) async-start(), calls=%async_computation.8 | async-start | bytes 1769472 | tf_op jit(solution)/shard_map/all_gather | solution.py:96
  82.5 18.0 %copy-start.10 = (s32[1024,1]{0,1:T(1,128)S(1)}, s32[1024,1]{0,1:T(1,128)}, u32[]{:S(2)}) copy-start(s32[1024,1]{0,1:T(1,128)} %get-tuple-element.348) | copy-start | bytes 12292
  86.0 9.3 %all-to-all-start.3 = ((bf16[4,24,2048]{2,1,0:T(8,128)(2,1)}), bf16[4,24,2048]{2,1,0:T(8,128)(2,1)S(1)}, u32[]{:S(2)}, u32[]{:S(2)}) async-start(bf16[4,24,2048]{2,1,0:T(8,128)(2,1)} %bitcast.15), calls=%async_computation.3 | async-start | bytes 786432 | tf_op jit(solution)/shard_map/all_to_all | solution.py:159
  95.3 26.5 %all-to-all-start.4 = ((bf16[128,8,256]{2,0,1:T(8,128)(2,1)}), bf16[128,8,256]{2,0,1:T(8,128)(2,1)S(1)}, u32[]{:S(2)}, u32[]{:S(2)}) async-start(bf16[128,8,256]{2,0,1:T(8,128)(2,1)} %get-tuple-element.350), calls=%async_computation.4 | async-start | bytes 1048576 | tf_op jit(solution)/shard_map/all_to_all | solution.py:89
  112.5 13.1 %copy-start.9 = (f32[128,8]{1,0:T(8,128)S(1)}, f32[128,8]{1,0:T(8,128)}, u32[]{:S(2)}) copy-start(f32[128,8]{1,0:T(8,128)} %copy-done.8) | copy-start | bytes 12292
  121.8 18.8 %all-to-all-start.5 = ((bf16[128,8,256]{2,0,1:T(8,128)(2,1)}), bf16[128,8,256]{2,0,1:T(8,128)(2,1)S(1)}, u32[]{:S(2)}, u32[]{:S(2)}) async-start(bf16[128,8,256]{2,0,1:T(8,128)(2,1)} %get-tuple-element.351), calls=%async_computation.5 | async-start | bytes 1048576 | tf_op jit(solution)/shard_map/all_to_all | solution.py:90
Sparse Core Ops, SparseCore 0:
  72.1 26.9 all-gather.3
  100.8 28.8 all-gather.5
  131.3 24.2 all-gather.7
where the time goes:
time: 166 us; the launch traced here: 165 us
  local copies, waits for them, and re-layouts  43.1 us (26%)
  waiting for transfers between devices  30.8 us (19%)
  other arithmetic  25.9 us (16%)
  starting transfers between devices  25.4 us (15%)
  matrix products  25.4 us (15%)
  between operations  14.8 us (9%)
    all_gather x1, waiting for transfers between devices, run_expert(): hidden_piece = lax.all_gather(hidden_all, 'dp', axis=0, tiled=True)  15.1 us
    reduce_sum x1, other arithmetic, per_device(): grad_tokens = jnp.sum(took_part, axis=1).astype(jnp.bfloat16)  10.4 us
    gather x1, local copies, waits for them, and re-layouts, per_device(): back_out.reshape(slot_total, model_width)[safe_slot].astype(jnp.float32)  6.03 us
    gather x1, local copies, waits for them, and re-layouts, per_device(): back_part.reshape(slot_total, model_width)[safe_slot].astype(jnp.float32)  6.01 us
    all_to_all x1, waiting for transfers between devices, run_expert(): lax.all_to_all(split_x, 'dp', split_axis=1, concat_axis=0, tiled=True)  5.3 us
    all_to_all x1, starting transfers between devices, per_device(): lax.all_to_all(send_x.reshape(held_count, CAP, model_width), 'expert', sp...  5.19 us
    all_to_all x1, starting transfers between devices, run_expert(): lax.all_to_all(split_x, 'dp', split_axis=1, concat_axis=0, tiled=True)  4.88 us
    gather x2, local copies, waits for them, and re-layouts, run_expert(): return (out_all[placement], part_all[placement], summed)  4.73 us
  transfers between devices with their start and end apart: 9, of which 6 were waited for; matrix products, arithmetic and copies ran while one was open for 32% of the time, Pallas kernels for 0%

commit v1 on v0

--- a/solution.py
+++ b/solution.py
@@ -93,7 +93,8 @@
     recv_dy = recv_dy.reshape(groups * padded_rows, width_part)
     gate_piece = lax.all_gather(gate_all, "dp", axis=0, tiled=True)
     up_piece = lax.all_gather(up_all, "dp", axis=0, tiled=True)
-    hidden_piece = lax.all_gather(hidden_all, "dp", axis=0, tiled=True)
+    repeated = jnp.stack([hidden_all] * lax.axis_size("dp"))
+    hidden_piece = jnp.concatenate(lax.all_to_all(repeated, "dp", 0, 0), axis=0)
     gate_term = lax.dot_general(
         recv_x, gate_piece, contract_first, preferred_element_type=jnp.float32
     )

time: 166 us -> 206 us (1.24)
  blocking collectives: 0 us -> 24.3 us
  waiting for transfers between devices: 30.8 us -> 46 us
    all_to_all x1, waiting for transfers between devices: 0.49 us -> 33.4 us  [run_expert(): hidden_piece = jnp.concatenate(lax.all_to_all(repeated, 'dp', 0, 0), axis=0)]
    all_to_all x0 -> x1, blocking collectives: none -> 24.3 us  [run_expert(): lax.all_to_all(split_dy, 'dp', split_axis=1, concat_axis=0, tiled=True)]
    all_gather x1 -> x0, waiting for transfers between devices: 15.1 us -> none  [run_expert(): hidden_piece = lax.all_gather(hidden_all, 'dp', axis=0, tiled=True)]
    all_to_all x1, waiting for transfers between devices: 5.3 us -> 2.58 us  [run_expert(): lax.all_to_all(split_x, 'dp', split_axis=1, concat_axis=0, tiled=True)]
    another operation x5 -> x6, local copies, waits for them, and re-layouts: 3.78 us -> 5.03 us
  transfers between devices with their start and end apart: 9 -> 8, of which waited for: 6 -> 5; matrix products, arithmetic and copies ran while one was open for 32% -> 25% of each run, Pallas kernels for 0% -> 0%
where the time goes in v1:
time: 206 us; the launch traced here: 205 us
  waiting for transfers between devices  46 us (22%)
  local copies, waits for them, and re-layouts  44.4 us (22%)
  matrix products  25.3 us (12%)
  other arithmetic  25.2 us (12%)
  starting transfers between devices  24.9 us (12%)
  blocking collectives  24.3 us (12%)
  between operations  15.1 us (7%)
    all_to_all x1, waiting for transfers between devices, run_expert(): hidden_piece = jnp.concatenate(lax.all_to_all(repeated, 'dp', 0, 0), axis=0)  33.4 us
    all_to_all x1, blocking collectives, run_expert(): lax.all_to_all(split_dy, 'dp', split_axis=1, concat_axis=0, tiled=True)  24.3 us
    reduce_sum x1, other arithmetic, per_device(): grad_tokens = jnp.sum(took_part, axis=1).astype(jnp.bfloat16)  10.4 us
    gather x1, local copies, waits for them, and re-layouts, per_device(): back_out.reshape(slot_total, model_width)[safe_slot].astype(jnp.float32)  6.03 us
    gather x1, local copies, waits for them, and re-layouts, per_device(): back_part.reshape(slot_total, model_width)[safe_slot].astype(jnp.float32)  6.01 us
    all_to_all x1, starting transfers between devices, per_device(): lax.all_to_all(send_x.reshape(held_count, CAP, model_width), 'expert', sp...  5.19 us
    gather x2, local copies, waits for them, and re-layouts, run_expert(): return (out_all[placement], part_all[placement], summed)  4.76 us
    all_to_all x1, waiting for transfers between devices, per_device(): lax.all_to_all(part_rows.reshape(held_count, CAP, model_width), 'expert',...  4.67 us
  transfers between devices with their start and end apart: 8, of which 5 were waited for; matrix products, arithmetic and copies ran while one was open for 25% of the time, Pallas kernels for 0%

profile of v1, /device:TPU:0, one launch (start us, length us, event | category | flops | bytes accessed | tf_op | source)
XLA Modules:
  0.0 205.2 jit_solution(18073316370430640707)
XLA Ops:
  11.8 4.3 %scatter_custom_fusion.1 = s32[96]{0:T(128)S(1)} fusion(s32[1024]{0:T(1024)S(1)} %bitcast.108, s32[1024]{0:T(1024)S(1)} %add_select_fusion, s32[]{:T(128)} %copy.53), kind=kCustom, calls=%fused_computation.100 | custom fusion | bytes 388 | tf_op jit(solution)/shard_map/scatter | solution.py:123
  16.1 4.3 %scatter_custom_fusion = pred[96]{0:T(512)(128)(4,1)S(1)} fusion(s32[1024]{0:T(1024)S(1)} %bitcast.109, pred[1024]{0:T(1024)(128)(4,1)S(1)} %broadcast.261, pred[]{:T(512)} %constant.84.clone.1), kind=kCustom, calls=%fused_computation.92 | custom fusion | bytes 97 | tf_op jit(solution)/shard_map/scatter | solution.py:129
  22.2 5.2 %all-to-all-start = ((bf16[4,24,2048]{2,1,0:T(8,128)(2,1)}), bf16[4,24,2048]{2,1,0:T(8,128)(2,1)S(1)}, u32[]{:S(2)}, u32[]{:S(2)}) async-start(bf16[4,24,2048]{2,1,0:T(8,128)(2,1)} %broadcast_select_fusion.1), calls=%async_computation | async-start | bytes 786432 | tf_op jit(solution)/shard_map/all_to_all | solution.py:133
  28.5 4.3 %scatter_custom_fusion.3 = f32[96]{0:T(128)S(1)} fusion(s32[1024]{0:T(1024)S(1)} %bitcast.110, f32[1024]{0:T(1024)S(1)} %reshape.416, f32[]{:T(128)} %constant.94.clone.1), kind=kCustom, calls=%fused_computation.95 | custom fusion | bytes 388 | tf_op jit(solution)/shard_map/scatter | solution.py:127
  34.0 3.9 %all-to-all-start.1 = ((bf16[4,24,2048]{2,1,0:T(8,128)(2,1)}), bf16[4,24,2048]{2,1,0:T(8,128)(2,1)S(1)}, u32[]{:S(2)}, u32[]{:S(2)}) async-start(bf16[4,24,2048]{2,1,0:T(8,128)(2,1)} %fusion.18), calls=%async_computation.1 | async-start | bytes 786432 | tf_op jit(solution)/shard_map/all_to_all | solution.py:140
  43.6 2.7 %negate_exponential_fusion = (f32[128,768]{1,0:T(8,128)S(1)}, f32[128,768]{1,0:T(8,128)S(1)}) fusion(bf16[2048,3,768]{2,0,1:T(8,128)(2,1)} %bitcast.111, bf16[128,2048]{1,0:T(8,128)(2,1)S(1)} %gather_fusion.1, pred[128]{0:T(512)(128)(4,1)S(1)} %iota_compare_fusion.2), kind=kOutput, calls=%fused_computation.56 | convolution fusion | flops 403013632 | bytes 4456576 | tf_op jit(solution)/shard_map/while/body/dot_general | solution.py:15
  49.8 3.5 %fusion.46 = (f32[128,768]{1,0:T(8,128)S(1)}, f32[128,768]{1,0:T(8,128)}) fusion(f32[128,768]{1,0:T(8,128)S(1)} %fusion.9, bf16[2048,3,768]{2,0,1:T(8,128)(2,1)} %bitcast.113, bf16[128,2048]{1,0:T(8,128)(2,1)S(1)} %gather_fusion.3, pred[128]{0:T(512)(128)(4,1)S(1)} %iota_compare_fusion.2), kind=kOutput, calls=%fused_computation.108 | convolution fusion | flops 403013632 | bytes 4849792 | tf_op jit(solution)/shard_map/while/body/dot_general | solution.py:23
  53.3 3.2 %fusion.14 = bf16[128,2048]{1,0:T(8,128)(2,1)S(1)} fusion(bf16[2048,3,768]{2,0,1:T(8,128)(2,1)} %bitcast.114, f32[128,768]{1,0:T(8,128)S(1)} %fusion.9, f32[128,768]{1,0:T(8,128)S(1)} %get-tuple-element.446), kind=kOutput, calls=%fused_computation.36 | convolution fusion | flops 403505152 | bytes 4456448 | tf_op jit(solution)/shard_map/while/body/dot_general | solution.py:20
  56.5 4.0 %fusion.6 = f32[128,2048]{1,0:T(8,128)} fusion(bf16[2048,3,768]{2,0,1:T(8,128)(2,1)} %bitcast.115, f32[128,768]{1,0:T(8,128)S(1)} %get-tuple-element.446, f32[128,768]{1,0:T(8,128)S(1)} %get-tuple-element.448), kind=kOutput, calls=%fused_computation.28 | convolution fusion | flops 403537920 | bytes 4980736 | tf_op jit(solution)/shard_map/while/body/dot_general | solution.py:29
  60.5 3.4 %fusion.13 = bf16[128,2048]{1,0:T(8,128)(2,1)S(1)} fusion(f32[128,2048]{1,0:T(8,128)} %fusion.6, bf16[2048,3,768]{2,0,1:T(8,128)(2,1)} %bitcast.116, f32[128,768]{1,0:T(8,128)} %get-tuple-element.449, f32[128,768]{1,0:T(8,128)S(1)} %get-tuple-element.446), kind=kOutput, calls=%fused_computation.35 | convolution fusion | flops 403767296 | bytes 5505024 | tf_op jit(solution)/shard_map/while/body/dot_general | solution.py:30
  67.7 3.6 %while.24 = (s32[]{:T(128)}, bf16[128,2048]{1,0:T(8,128)(2,1)}, bf16[128,2048]{1,0:T(8,128)(2,1)}, bf16[128,768]{1,0:T(8,128)(2,1)}, bf16[128,768]{1,0:T(8,128)(...) while((s32[]{:T(128)}, bf16[128,2048]{1,0:T(8,128)(2,1)}, ...), condition=%wide.region_12.13_spmd, body=%wide.region_11.12_spmd.sunk | while | flops 1277954 | bytes 4653197 | solution.py:80
  71.4 3.2 %gather_fusion.4 = bf16[96,2048]{1,0:T(8,128)(2,1)} fusion(bf16[128,2048]{1,0:T(8,128)(2,1)} %get-tuple-element.306, s32[1024]{0:T(1024)S(1)} %pad_clamp_fusion), kind=kCustom, calls=%fused_computation.4 | custom fusion | bytes 786816 | tf_op jit(solution)/shard_map/gather | solution.py:107
  74.6 4.3 %all-to-all-start.2 = ((bf16[4,24,2048]{2,1,0:T(8,128)(2,1)}), bf16[4,24,2048]{2,1,0:T(8,128)(2,1)S(1)}, u32[]{:S(2)}, u32[]{:S(2)}) async-start(bf16[4,24,2048]{2,1,0:T(8,128)(2,1)} %bitcast.101), calls=%async_computation.2 | async-start | bytes 786432 | tf_op jit(solution)/shard_map/all_to_all | solution.py:153
  81.2 3.6 %all-to-all-done.2 = bf16[4,24,2048]{2,1,0:T(8,128)(2,1)S(1)} async-done(((bf16[4,24,2048]{2,1,0:T(8,128)(2,1)}), bf16[4,24,2048]{2,1,0:T(8,128)(2,1)S(1)}, u32[]{:S(2)}, u32[]{:S(2)}) %all-to-all-start.2) | async-done | bytes 393248 | tf_op jit(solution)/shard_map/all_to_all | solution.py:153
  84.8 3.5 %all-to-all-start.3 = ((bf16[4,24,2048]{2,1,0:T(8,128)(2,1)}), bf16[4,24,2048]{2,1,0:T(8,128)(2,1)S(1)}, u32[]{:S(2)}, u32[]{:S(2)}) async-start(bf16[4,24,2048]{2,1,0:T(8,128)(2,1)} %bitcast.102), calls=%async_computation.3 | async-start | bytes 786432 | tf_op jit(solution)/shard_map/all_to_all | solution.py:160
  89.4 4.7 %all-to-all-done.3 = bf16[4,24,2048]{2,1,0:T(8,128)(2,1)S(1)} async-done(((bf16[4,24,2048]{2,1,0:T(8,128)(2,1)}), bf16[4,24,2048]{2,1,0:T(8,128)(2,1)S(1)}, u32[]{:S(2)}, u32[]{:S(2)}) %all-to-all-start.3) | async-done | bytes 393248 | tf_op jit(solution)/shard_map/all_to_all | solution.py:160
  94.1 24.3 %all_to_all.55 = bf16[128,8,256]{2,0,1:T(8,128)(2,1)} all-to-all(bf16[128,8,256]{2,0,1:T(8,128)(2,1)} %get-tuple-element.351), channel_id=1, replica_groups=mesh['dp'=8,'expert'=4] {'dp'}, dimensions={1} | all-to-all | bytes 1048576 | tf_op jit(solution)/shard_map/all_to_all | solution.py:90
  119.6 4.3 %all-to-all-start.6 = ((bf16[8,128,768]{2,1,0:T(8,128)(2,1)}), bf16[8,128,768]{2,1,0:T(8,128)(2,1)}, u32[]{:S(2)}, u32[]{:S(2)}) async-start(bf16[8,128,768]{2,1,0:T(8,128)(2,1)} %stack.12), calls=%async_computation.6 | async-start | bytes 3145728 | tf_op jit(solution)/shard_map/all_to_all | solution.py:97
  124.9 6.0 %gather_fusion.5 = bf16[1024,2048]{1,0:T(8,128)(2,1)} fusion(bf16[96,2048]{1,0:T(8,128)(2,1)S(1)} %bitcast.92, s32[1024]{0:T(1024)S(1)} %broadcast_clamp_fusion), kind=kCustom, calls=%fused_computation.5 | custom fusion | bytes 8392704 | tf_op jit(solution)/shard_map/gather | solution.py:171
  130.9 6.0 %gather_fusion.7 = bf16[1024,2048]{1,0:T(8,128)(2,1)} fusion(bf16[96,2048]{1,0:T(8,128)(2,1)S(1)} %bitcast.93, s32[1024]{0:T(1024)S(1)} %broadcast_clamp_fusion), kind=kCustom, calls=%fused_computation.7 | custom fusion | bytes 8392704 | tf_op jit(solution)/shard_map/gather | solution.py:176
  136.9 3.2 %fusion.4 = f32[1024]{0:T(1024)S(1)} fusion(bf16[1024,2048]{1,0:T(8,128)(2,1)} %gather_fusion.5, f32[128,2048]{1,0:T(8,128)S(1)} %convert_element_type.142, pred[1024]{0:T(1024)(128)(4,1)S(1)} %broadcast_in_dim.103), kind=kLoop, calls=%fused_computation.22 | loop fusion | flops 8387584 | bytes 5248000 | tf_op jit(solution)/shard_map/reduce_sum | solution.py:180
  140.9 33.4 %all-to-all-done.6 = bf16[8,128,768]{2,1,0:T(8,128)(2,1)} async-done(((bf16[8,128,768]{2,1,0:T(8,128)(2,1)}), bf16[8,128,768]{2,1,0:T(8,128)(2,1)}, u32[]{:S(2)}, u32[]{:S(2)}) %all-to-all-start.6) | async-done | bytes 1572896 | tf_op jit(solution)/shard_map/all_to_all | solution.py:97
  174.4 3.7 %all-to-all-start.4 = ((bf16[128,8,256]{2,0,1:T(8,128)(2,1)}), bf16[128,8,256]{2,0,1:T(8,128)(2,1)S(1)}, u32[]{:S(2)}, u32[]{:S(2)}) async-start(bf16[128,8,256]{2,0,1:T(8,128)(2,1)} %get-tuple-element.350), calls=%async_computation.4 | async-start | bytes 1048576 | tf_op jit(solution)/shard_map/all_to_all | solution.py:89
  178.1 10.4 %fusion.5 = (bf16[128,2048]{1,0:T(8,128)(2,1)}, bf16[128,2048]{1,0:T(8,128)(2,1)}) fusion(bf16[1024,2048]{1,0:T(8,128)(2,1)} %gather_fusion.7, pred[128,8]{1,0:T(8,128)(4,1)S(1)} %copy.15, bf16[1024,2048]{1,0:T(8,128)(2,1)} %gather_fusion.5, f32[128,8]{1,0:T(8,128)S(1)} %copy.14), kind=kLoop, calls=%fused_computation.24 | loop fusion | flops 14155776 | bytes 9442304 | tf_op jit(solution)/shard_map/reduce_sum | solution.py:181
  (100 shorter events, 40.6 us)
Async XLA Ops:
  7.2 13.4 %copy-start = (bf16[128,2048]{1,0:T(8,128)(2,1)S(1)}, bf16[128,2048]{1,0:T(8,128)(2,1)}, u32[]{:S(2)}) copy-start(bf16[128,2048]{1,0:T(8,128)(2,1)} %param.7) | copy-start | bytes 1572868
  7.2 20.2 %copy-start.1 = (bf16[128,2048]{1,0:T(8,128)(2,1)S(1)}, bf16[128,2048]{1,0:T(8,128)(2,1)}, u32[]{:S(2)}) copy-start(bf16[128,2048]{1,0:T(8,128)(2,1)} %param.10) | copy-start | bytes 1572868
  20.5 7.7 %copy-start.10 = (f32[128,8]{0,1:T(8,128)S(1)}, f32[128,8]{0,1:T(8,128)}, u32[]{:S(2)}) copy-start(f32[128,8]{0,1:T(8,128)} %param.9) | copy-start | bytes 12292
  22.2 11.8 %all-to-all-start = ((bf16[4,24,2048]{2,1,0:T(8,128)(2,1)}), bf16[4,24,2048]{2,1,0:T(8,128)(2,1)S(1)}, u32[]{:S(2)}, u32[]{:S(2)}) async-start(bf16[4,24,2048]{2,1,0:T(8,128)(2,1)} %broadcast_select_fusion.1), calls=%async_computation | async-start | bytes 786432 | tf_op jit(solution)/shard_map/all_to_all | solution.py:133
  34.0 14.8 %all-to-all-start.1 = ((bf16[4,24,2048]{2,1,0:T(8,128)(2,1)}), bf16[4,24,2048]{2,1,0:T(8,128)(2,1)S(1)}, u32[]{:S(2)}, u32[]{:S(2)}) async-start(bf16[4,24,2048]{2,1,0:T(8,128)(2,1)} %fusion.18), calls=%async_computation.1 | async-start | bytes 786432 | tf_op jit(solution)/shard_map/all_to_all | solution.py:140
  43.6 5.3 %copy-start.4 = (bf16[128,2048]{1,0:T(8,128)(2,1)}, bf16[128,2048]{1,0:T(8,128)(2,1)S(1)}, u32[]{:S(2)}) copy-start(bf16[128,2048]{1,0:T(8,128)(2,1)S(1)} %gather_fusion.1) | copy-start | bytes 1572868
  49.8 3.5 %copy-start.6 = (bf16[128,2048]{1,0:T(8,128)(2,1)}, bf16[128,2048]{1,0:T(8,128)(2,1)S(1)}, u32[]{:S(2)}) copy-start(bf16[128,2048]{1,0:T(8,128)(2,1)S(1)} %gather_fusion.3) | copy-start | bytes 1572868
  53.3 3.2 %copy-start.3 = (f32[128,768]{1,0:T(8,128)}, f32[128,768]{1,0:T(8,128)S(1)}, u32[]{:S(2)}) copy-start(f32[128,768]{1,0:T(8,128)S(1)} %get-tuple-element.448) | copy-start | bytes 1179652
  71.4 8.2 %copy-start.2 = (bf16[128,2048]{1,0:T(8,128)(2,1)S(1)}, bf16[128,2048]{1,0:T(8,128)(2,1)}, u32[]{:S(2)}) copy-start(bf16[128,2048]{1,0:T(8,128)(2,1)} %get-tuple-element.307) | copy-start | bytes 1572868
  71.4 16.9 %copy-start.5 = (bf16[128,2048]{1,0:T(8,128)(2,1)S(1)}, bf16[128,2048]{1,0:T(8,128)(2,1)}, u32[]{:S(2)}) copy-start(bf16[128,2048]{1,0:T(8,128)(2,1)} %copy-done.4) | copy-start | bytes 1572868
  71.4 16.9 %copy-start.7 = (bf16[128,2048]{1,0:T(8,128)(2,1)S(1)}, bf16[128,2048]{1,0:T(8,128)(2,1)}, u32[]{:S(2)}) copy-start(bf16[128,2048]{1,0:T(8,128)(2,1)} %copy-done.6) | copy-start | bytes 1572868
  74.6 43.8 %copy-start.9 = (bf16[128,768]{1,0:T(8,128)(2,1)S(1)}, bf16[128,768]{1,0:T(8,128)(2,1)}, u32[]{:S(2)}) copy-start(bf16[128,768]{1,0:T(8,128)(2,1)} %get-tuple-element.310) | copy-start | bytes 589828
  74.6 10.2 %all-to-all-start.2 = ((bf16[4,24,2048]{2,1,0:T(8,128)(2,1)}), bf16[4,24,2048]{2,1,0:T(8,128)(2,1)S(1)}, u32[]{:S(2)}, u32[]{:S(2)}) async-start(bf16[4,24,2048]{2,1,0:T(8,128)(2,1)} %bitcast.101), calls=%async_computation.2 | async-start | bytes 786432 | tf_op jit(solution)/shard_map/all_to_all | solution.py:153
  78.9 114.2 %all-gather.3.cloned.1.call-start = ((), (), s32[]{:S(2)}) async-start(), calls=%async_computation.7 | async-start | bytes 1769472 | tf_op jit(solution)/shard_map/all_gather | solution.py:94
  84.8 9.3 %all-to-all-start.3 = ((bf16[4,24,2048]{2,1,0:T(8,128)(2,1)}), bf16[4,24,2048]{2,1,0:T(8,128)(2,1)S(1)}, u32[]{:S(2)}, u32[]{:S(2)}) async-start(bf16[4,24,2048]{2,1,0:T(8,128)(2,1)} %bitcast.102), calls=%async_computation.3 | async-start | bytes 786432 | tf_op jit(solution)/shard_map/all_to_all | solution.py:160
  119.6 54.7 %all-to-all-start.6 = ((bf16[8,128,768]{2,1,0:T(8,128)(2,1)}), bf16[8,128,768]{2,1,0:T(8,128)(2,1)}, u32[]{:S(2)}, u32[]{:S(2)}) async-start(bf16[8,128,768]{2,1,0:T(8,128)(2,1)} %stack.12), calls=%async_computation.6 | async-start | bytes 3145728 | tf_op jit(solution)/shard_map/all_to_all | solution.py:97
  123.9 71.2 %all-gather.5.cloned.1.call-start = ((), (), s32[]{:S(2)}) async-start(), calls=%async_computation.8 | async-start | bytes 1769472 | tf_op jit(solution)/shard_map/all_gather | solution.py:95
  174.4 18.8 %all-to-all-start.4 = ((bf16[128,8,256]{2,0,1:T(8,128)(2,1)}), bf16[128,8,256]{2,0,1:T(8,128)(2,1)S(1)}, u32[]{:S(2)}, u32[]{:S(2)}) async-start(bf16[128,8,256]{2,0,1:T(8,128)(2,1)} %get-tuple-element.350), calls=%async_computation.4 | async-start | bytes 1048576 | tf_op jit(solution)/shard_map/all_to_all | solution.py:89
  178.1 10.4 %copy-start.8 = (bf16[128,8,256]{2,0,1:T(8,128)(2,1)S(1)}, bf16[128,8,256]{2,0,1:T(8,128)(2,1)}, u32[]{:S(2)}) copy-start(bf16[128,8,256]{2,0,1:T(8,128)(2,1)} %all_to_all.55) | copy-start | bytes 1572868
Sparse Core Ops, SparseCore 0:
  81.3 31.5 all-gather.2
  126.4 44.4 all-gather.4
